TPU v7x, 256 devices: a whole 4x4x8 slice. The times are simulated.
256 devices in a mesh: section: 2 (over y_hi), seq: 32 (over x, z), chan: 4 (over y_lo, core).
Axes of the slice: x: 4, y: 4 (y_hi: 2, y_lo: 2; y = y_hi * 2 + y_lo), z: 8, core: 2. Of those that a mesh axis runs over, the one named last changes fastest.
Arguments:
- bases: int32 [2, 2097152], P('section', 'seq'), may hold values from 0 to 3
- stem_embedding_weight: bfloat16 [512, 1536], P(None, 'chan'), may hold values from -1.64443437 to 1.64443437
- gains: float32 [3, 1536], replicated, may hold values from 0.1 to 1.9
- conv_weight: bfloat16 [3, 3, 1536, 1536], P(None, None, None, 'chan'), may hold values from -0.09375 to 0.09375
- dec_weight: bfloat16 [1536, 384], P('chan'), may hold values from -0.3125 to 0.3125
- upstream: bfloat16 [2, 16384, 1536], P('section', 'seq', 'chan'), may hold values from -0.032958984 to 0.032958984
Outputs:
- decoded: bfloat16 [2, 16384, 1536], P('section', 'seq', 'chan')
- weight_grad: float32 [1536, 384], P('chan')
All inputs are finite; a program needn't handle non-finite values.
Results may differ from a plain program's by a relative error of at most 0.0076.
Values may be sent and summed in bfloat16 or wider, within the bound.
No kernel may reach another device: no remote copies, remote signals or barrier semaphores. Data moves between devices by JAX's collectives and lax.ppermute only.
A program may use at most 128 MiB of HBM per device.

v0:
```python
import jax
import jax.numpy as jnp
from jax import lax
from jax.sharding import PartitionSpec as P

PATCH = 128
FIRST_DILATION0 = 2
EPSILON = 1e-06


def with_halo(shard, sides, width):
    for axis, dim in sides:
        size, length = (lax.axis_size(axis), shard.shape[dim])
        up = [(i, (i + 1) % size) for i in range(size - 1)]
        down = [(j, i) for i, j in up]
        last = lax.slice_in_dim(shard, length - width, length, axis=dim)
        initial = lax.slice_in_dim(shard, 0, width, axis=dim)
        before = lax.ppermute(last, axis, up)
        after = lax.ppermute(initial, axis, down)
        shard = jnp.concatenate([before, shard, after], axis=dim)
    return shard


def activate(rows, gain_row):
    widened = rows.astype(jnp.float32)
    inverse_rms = lax.rsqrt(jnp.mean(widened * widened, axis=-1, keepdims=True) + EPSILON)
    return jax.nn.gelu(widened * inverse_rms * gain_row).astype(jnp.bfloat16)


def apply_convolution(padded, kernel_taps, dilation_step, row_count):
    update = jnp.dot(padded[0:row_count], kernel_taps[0], preferred_element_type=jnp.float32)
    for offset in range(1, kernel_taps.shape[0]):
        start = offset * dilation_step
        update = update + jnp.dot(
            padded[start : start + row_count],
            kernel_taps[offset],
            preferred_element_type=jnp.float32,
        )
    return update


def body(bases, stem_embedding_weight, gains, conv_weight, dec_weight, upstream):
    row_count = upstream.shape[1]
    letters = bases.reshape(row_count, PATCH)
    onehot = letters[:, :, None] == jnp.arange(4, dtype=jnp.int32)[None, None, :]
    onehot = onehot.astype(jnp.bfloat16).reshape(row_count, PATCH * 4)
    stream = jnp.dot(onehot, stem_embedding_weight, preferred_element_type=jnp.float32).astype(
        jnp.bfloat16
    )
    for tower_layer_index in range(conv_weight.shape[0]):
        dilation_step = FIRST_DILATION0 * 2**tower_layer_index
        full_rows = lax.all_gather(stream, "chan", axis=1, tiled=True)
        padded = with_halo(
            activate(full_rows, gains[tower_layer_index]), (("seq", 0),), dilation_step
        )
        update = apply_convolution(padded, conv_weight[tower_layer_index], dilation_step, row_count)
        stream = (stream.astype(jnp.float32) + update).astype(jnp.bfloat16)
    decoded = jnp.dot(stream, dec_weight, preferred_element_type=jnp.float32).astype(jnp.bfloat16)
    upstream_rows = upstream[0]
    contract_row_pairs = (((0,), (0,)), ((), ()))
    partial_grad = lax.dot_general(
        stream, upstream_rows, contract_row_pairs, preferred_element_type=jnp.float32
    )
    weight_grad = lax.psum(partial_grad, ("section", "seq"))
    return (decoded[None], weight_grad)


def solution(mesh):
    placed = (
        P("section", "seq"),
        P(None, "chan"),
        P(),
        P(None, None, None, "chan"),
        P("chan", None),
        P("section", "seq", "chan"),
    )
    return jax.shard_map(
        body,
        mesh=mesh,
        in_specs=placed,
        out_specs=(P("section", "seq", "chan"), P("chan", None)),
        check_vma=False,
    )
```

profile of v0, /device:TPU:24, one launch (start us, length us, event | category | flops | bytes accessed | tf_op | source)
XLA Modules:
  0.0 813.8 jit_solution(4729358638135030658)
XLA Ops:
  7.2 0.0 copy-start
  7.2 0.0 all-gather.4.cloned.1.call-start
  7.2 0.1 eq.26
  7.4 1.1 copy.8
  8.4 0.2 eq.23
  8.6 0.4 eq.24
  9.0 1.3 convolution_convert_fusion.1
  10.3 0.0 all-gather.4.cloned.1.call-update
  10.4 0.0 all-gather.6.cloned.1.call-start
  10.4 0.1 slice_reduce_fusion
  10.5 29.4 %all-gather.4.cloned.1.call-done = bf16[512,1536]{1,0:T(8,128)(2,1)} async-done(((bf16[512,384]{1,0:T(8,128)(2,1)}), bf16[512,1536]{1,0:T(8,128)(2,1)}) %all-gather.4.cloned.1.call-update) | async-done | bytes 1572880 | tf_op jit(solution)/shard_map/all_gather | solution.py:52
  39.8 1.8 fusion
  41.6 2.8 fusion.4
  44.5 3.5 collective-permute-start
  47.9 1.3 collective-permute-start.1
  49.2 2.2 fusion.60
  51.5 0.0 copy-start.1
  51.5 2.0 collective-permute-done.1
  53.4 2.3 fusion.38
  55.7 3.1 fusion.49
  58.8 0.0 all-gather.6.cloned.1.call-update
  58.8 0.0 all-gather.8.cloned.1.call-start
  58.8 28.8 %all-gather.6.cloned.1.call-done = bf16[512,1536]{1,0:T(8,128)(2,1)} async-done(((bf16[512,384]{1,0:T(8,128)(2,1)}), bf16[512,1536]{1,0:T(8,128)(2,1)}) %all-gather.6.cloned.1.call-update) | async-done | bytes 1572880 | tf_op jit(solution)/shard_map/all_gather | solution.py:52
  87.6 1.8 fusion.9
  89.4 2.8 fusion.13
  92.2 1.3 collective-permute-start.3
  93.5 2.2 fusion.56
  95.8 0.0 copy-start.3
  95.8 4.7 collective-permute-start.2
  100.5 2.3 fusion.34
  102.8 3.0 add_convert_fusion.1
  105.8 0.0 all-gather.8.cloned.1.call-update
  105.9 0.0 all-reduce.2.cloned.1.call-start
  105.9 29.4 %all-gather.8.cloned.1.call-done = bf16[512,1536]{1,0:T(8,128)(2,1)} async-done(((bf16[512,384]{1,0:T(8,128)(2,1)}), bf16[512,1536]{1,0:T(8,128)(2,1)}) %all-gather.8.cloned.1.call-update) | async-done | bytes 1572880 | tf_op jit(solution)/shard_map/all_gather | solution.py:52
  135.3 1.8 fusion.18
  137.1 2.8 fusion.22
  139.9 1.5 collective-permute-start.5
  141.4 2.2 fusion.52
  143.7 0.0 copy-start.2
  143.7 4.7 collective-permute-start.4
  148.4 2.2 fusion.30
  150.6 0.0 copy-start.5
  150.7 2.3 add_convert_fusion
  153.0 1.2 fusion.74
  154.3 0.0 all-reduce.2.cloned.1.call-update
  154.3 1.1 fusion.50
  155.4 649.9 %all-reduce.2.cloned.1.call-done = f32[384,384]{1,0:T(8,128)} async-done(((f32[384,384]{1,0:T(8,128)}), f32[384,384]{1,0:T(8,128)}) %all-reduce.2.cloned.1.call-update) | async-done | bytes 589840 | tf_op jit(solution)/shard_map/psum | solution.py:64
  805.3 1.9 copy.10
  (21 shorter events, 0.1 us)
Async XLA Ops:
  7.2 1.8 copy-start
  7.2 3.2 copy-start.6
  7.2 32.7 %all-gather.4.cloned.1.call-start = ((), (), s32[]{:S(2)}) async-start(), calls=%async_computation | async-start | bytes 1966080 | tf_op jit(solution)/shard_map/all_gather | solution.py:52
  10.4 77.3 %all-gather.6.cloned.1.call-start = ((), (), s32[]{:S(2)}) async-start(), calls=%async_computation.1 | async-start | bytes 1966080 | tf_op jit(solution)/shard_map/all_gather | solution.py:52
  44.5 11.2 %collective-permute-start = (bf16[2,1536]{1,0:T(2,128)(2,1)S(1)}, bf16[2,1536]{1,0:T(2,128)(2,1)S(1)}, u32[]{:S(2)}, u32[]{:S(2)}) collective-permute-start(bf16[2,1536]{1,0:T(2,128)(2,1)S(1)} %get-tuple-element.9), channel_id=1, source_target_pairs={{0,4},{4,8},{8,12},{12,16},{16,20},{20,24},{24,28},{28,32},{32,36}... | collective-permute-start | bytes 18440 | tf_op jit(solution)/shard_map/ppermute | solution.py:18
  47.9 5.5 collective-permute-start.1
  51.5 4.2 copy-start.1
  58.8 76.5 %all-gather.8.cloned.1.call-start = ((), (), s32[]{:S(2)}) async-start(), calls=%async_computation.2 | async-start | bytes 1966080 | tf_op jit(solution)/shard_map/all_gather | solution.py:52
  92.2 8.3 %collective-permute-start.3 = (bf16[4,1536]{1,0:T(4,128)(2,1)S(1)}, bf16[4,1536]{1,0:T(4,128)(2,1)S(1)}, u32[]{:S(2)}, u32[]{:S(2)}) collective-permute-start(bf16[4,1536]{1,0:T(4,128)(2,1)S(1)} %get-tuple-element.8), channel_id=1, source_target_pairs={{4,0},{8,4},{12,8},{16,12},{20,16},{24,20},{28,24},{32,28},{36,32}... | collective-permute-start | bytes 36872 | tf_op jit(solution)/shard_map/ppermute | solution.py:19
  95.8 7.0 copy-start.3
  95.8 7.0 collective-permute-start.2
  105.9 699.5 %all-reduce.2.cloned.1.call-start = ((), (), s32[]{:S(2)}) async-start(), calls=%async_computation.3 | async-start | bytes 1179648 | tf_op jit(solution)/shard_map/psum | solution.py:64
  139.9 8.4 %collective-permute-start.5 = (bf16[8,1536]{1,0:T(8,128)(2,1)S(1)}, bf16[8,1536]{1,0:T(8,128)(2,1)S(1)}, u32[]{:S(2)}, u32[]{:S(2)}) collective-permute-start(bf16[8,1536]{1,0:T(8,128)(2,1)S(1)} %get-tuple-element.6), channel_id=1, source_target_pairs={{4,0},{8,4},{12,8},{16,12},{20,16},{24,20},{28,24},{32,28},{36,32}... | collective-permute-start | bytes 73736 | tf_op jit(solution)/shard_map/ppermute | solution.py:19
  143.7 7.0 copy-start.2
  143.7 7.0 collective-permute-start.4
  150.6 2.4 copy-start.4
  150.6 3.6 copy-start.5
Sparse Core Ops, SparseCore 0:
  10.5 29.3 all-gather.3
  58.9 28.6 all-gather.5
  106.0 29.3 all-gather.7
  154.4 650.8 all-reduce.1
where the time goes:
time: 815 us; the launch traced here: 814 us
  waiting for transfers between devices  740 us (91%)
  matrix products  25.6 us (3%)
  starting transfers between devices  17 us (2%)
  between operations  14.1 us (2%)
  other arithmetic  13.7 us (2%)
    psum x1, waiting for transfers between devices, body(): weight_grad = lax.psum(partial_grad, ('section', 'seq'))  650 us
    all_gather x3, waiting for transfers between devices, body(): full_rows = lax.all_gather(stream, 'chan', axis=1, tiled=True)  87.6 us
  transfers between devices with their start and end apart: 10, of which 5 were waited for; matrix products, arithmetic and copies ran while one was open for 2% of the time, Pallas kernels for 0%

commit v1 on v0

--- a/solution.py
+++ b/solution.py
@@ -61,7 +61,7 @@
     partial_grad = lax.dot_general(
         stream, upstream_rows, contract_row_pairs, preferred_element_type=jnp.float32
     )
-    weight_grad = lax.psum(partial_grad, ("section", "seq"))
+    weight_grad = jnp.sum(lax.all_gather(partial_grad, ("section", "seq")), axis=0)
     return (decoded[None], weight_grad)
 
 

time: 815 us -> 532 us (0.65)
  waiting for transfers between devices: 740 us -> 443 us
  other arithmetic: 13.7 us -> 27.9 us
    psum x1 -> x0, waiting for transfers between devices: 650 us -> none  [body(): weight_grad = lax.psum(partial_grad, ('section', 'seq'))]
    all_gather x0 -> x1, waiting for transfers between devices: none -> 353 us  [body(): lax.all_gather(partial_grad, ('section', 'seq'))]
    reduce_sum x0 -> x1, other arithmetic: none -> 14.1 us  [body(): jnp.sum(lax.all_gather(partial_grad, ('section', 'seq')), axis=0)]
  transfers between devices with their start and end apart: 10 -> 10, of which waited for: 5 -> 5; matrix products, arithmetic and copies ran while one was open for 2% -> 3% of each run, Pallas kernels for 0% -> 0%
where the time goes in v1:
time: 532 us; the launch traced here: 529 us
  waiting for transfers between devices  443 us (83%)
  other arithmetic  27.9 us (5%)
  matrix products  25.6 us (5%)
  starting transfers between devices  17 us (3%)
  between operations  14.1 us (3%)
    all_gather x1, waiting for transfers between devices, body(): lax.all_gather(partial_grad, ('section', 'seq'))  353 us
    all_gather x3, waiting for transfers between devices, body(): full_rows = lax.all_gather(stream, 'chan', axis=1, tiled=True)  87.6 us
    reduce_sum x1, other arithmetic, body(): jnp.sum(lax.all_gather(partial_grad, ('section', 'seq')), axis=0)  14.1 us
    dot_general x6, matrix products, apply_convolution(): jnp.dot(padded[start:start + row_count], kernel_taps[offset], preferred_e...  13.5 us
    ppermute x3, starting transfers between devices, with_halo(): before = lax.ppermute(last, axis, up)  12.8 us
  transfers between devices with their start and end apart: 10, of which 5 were waited for; matrix products, arithmetic and copies ran while one was open for 3% of the time, Pallas kernels for 0%

profile of v1, /device:TPU:24, one launch (start us, length us, event | category | flops | bytes accessed | tf_op | source)
XLA Modules:
  0.0 529.1 jit_solution(6820795464893698286)
XLA Ops:
  7.2 0.0 copy-start
  7.2 0.0 all-gather.6.cloned.1.call-start
  7.3 0.1 eq.26
  7.4 1.1 copy.8
  8.4 0.2 eq.23
  8.6 0.4 eq.24
  9.0 1.3 convolution_convert_fusion.1
  10.3 0.0 all-gather.6.cloned.1.call-update
  10.4 0.0 all-gather.8.cloned.1.call-start
  10.4 0.1 slice_reduce_fusion
  10.5 29.4 %all-gather.6.cloned.1.call-done = bf16[512,1536]{1,0:T(8,128)(2,1)} async-done(((bf16[512,384]{1,0:T(8,128)(2,1)}), bf16[512,1536]{1,0:T(8,128)(2,1)}) %all-gather.6.cloned.1.call-update) | async-done | bytes 1572880 | tf_op jit(solution)/shard_map/all_gather | solution.py:52
  39.8 1.8 fusion
  41.6 2.8 fusion.4
  44.5 3.5 collective-permute-start
  47.9 1.3 collective-permute-start.1
  49.2 2.2 fusion.60
  51.5 0.0 copy-start.2
  51.5 2.0 collective-permute-done.1
  53.4 2.3 fusion.38
  55.7 3.1 fusion.49
  58.8 0.0 all-gather.8.cloned.1.call-update
  58.8 0.0 all-gather.10.cloned.1.call-start
  58.8 28.8 %all-gather.8.cloned.1.call-done = bf16[512,1536]{1,0:T(8,128)(2,1)} async-done(((bf16[512,384]{1,0:T(8,128)(2,1)}), bf16[512,1536]{1,0:T(8,128)(2,1)}) %all-gather.8.cloned.1.call-update) | async-done | bytes 1572880 | tf_op jit(solution)/shard_map/all_gather | solution.py:52
  87.6 1.8 fusion.9
  89.4 2.8 fusion.13
  92.2 1.3 collective-permute-start.3
  93.5 2.2 fusion.56
  95.8 0.0 copy-start.4
  95.8 4.7 collective-permute-start.2
  100.5 2.3 fusion.34
  102.8 3.1 add_convert_fusion.1
  105.9 0.0 all-gather.10.cloned.1.call-update
  105.9 0.0 all-gather.12.cloned.1.call-start
  105.9 29.4 %all-gather.10.cloned.1.call-done = bf16[512,1536]{1,0:T(8,128)(2,1)} async-done(((bf16[512,384]{1,0:T(8,128)(2,1)}), bf16[512,1536]{1,0:T(8,128)(2,1)}) %all-gather.10.cloned.1.call-update) | async-done | bytes 1572880 | tf_op jit(solution)/shard_map/all_gather | solution.py:52
  135.4 1.8 fusion.18
  137.2 2.8 fusion.22
  140.0 1.5 collective-permute-start.5
  141.4 2.2 fusion.52
  143.7 0.0 copy-start.3
  143.7 4.7 collective-permute-start.4
  148.4 2.2 fusion.30
  150.7 0.0 copy-start.6
  150.7 2.3 add_convert_fusion
  153.1 1.2 fusion.74
  154.3 0.0 all-gather.12.cloned.1.call-update
  154.3 1.1 fusion.50
  155.5 353.0 %all-gather.12.cloned.1.call-done = f32[24576,384]{1,0:T(8,128)} async-done(((f32[384,384]{1,0:T(8,128)}), f32[24576,384]{1,0:T(8,128)}) %all-gather.12.cloned.1.call-update) | async-done | bytes 37748752 | tf_op jit(solution)/shard_map/all_gather | solution.py:64
  508.5 14.1 %reduce_sum.39 = f32[384,384]{1,0:T(8,128)} reduce(f32[64,384,384]{2,1,0:T(8,128)} %bitcast.47, f32[]{:T(128)} %constant.3.clone.1), dimensions={0}, to_apply=%region_3.0 | reduce | flops 9289728 | bytes 38338564 | tf_op jit(solution)/shard_map/reduce_sum | solution.py:64
  (23 shorter events, 0.1 us)
Async XLA Ops:
  7.2 1.8 copy-start
  7.2 3.2 copy-start.7
  7.2 32.7 %all-gather.6.cloned.1.call-start = ((), (), s32[]{:S(2)}) async-start(), calls=%async_computation | async-start | bytes 1966080 | tf_op jit(solution)/shard_map/all_gather | solution.py:52
  10.4 77.3 %all-gather.8.cloned.1.call-start = ((), (), s32[]{:S(2)}) async-start(), calls=%async_computation.1 | async-start | bytes 1966080 | tf_op jit(solution)/shard_map/all_gather | solution.py:52
  44.5 11.2 %collective-permute-start = (bf16[2,1536]{1,0:T(2,128)(2,1)S(1)}, bf16[2,1536]{1,0:T(2,128)(2,1)S(1)}, u32[]{:S(2)}, u32[]{:S(2)}) collective-permute-start(bf16[2,1536]{1,0:T(2,128)(2,1)S(1)} %get-tuple-element.9), channel_id=1, source_target_pairs={{0,4},{4,8},{8,12},{12,16},{16,20},{20,24},{24,28},{28,32},{32,36}... | collective-permute-start | bytes 18440 | tf_op jit(solution)/shard_map/ppermute | solution.py:18
  47.9 5.5 %collective-permute-start.1 = (bf16[2,1536]{1,0:T(2,128)(2,1)S(1)}, bf16[2,1536]{1,0:T(2,128)(2,1)S(1)}, u32[]{:S(2)}, u32[]{:S(2)}) collective-permute-start(bf16[2,1536]{1,0:T(2,128)(2,1)S(1)} %get-tuple-element.10), channel_id=1, source_target_pairs={{4,0},{8,4},{12,8},{16,12},{20,16},{24,20},{28,24},{32,28},{36,32}... | collective-permute-start | bytes 18440 | tf_op jit(solution)/shard_map/ppermute | solution.py:19
  51.5 4.2 copy-start.2
  58.8 76.6 %all-gather.10.cloned.1.call-start = ((), (), s32[]{:S(2)}) async-start(), calls=%async_computation.2 | async-start | bytes 1966080 | tf_op jit(solution)/shard_map/all_gather | solution.py:52
  92.2 8.2 %collective-permute-start.3 = (bf16[4,1536]{1,0:T(4,128)(2,1)S(1)}, bf16[4,1536]{1,0:T(4,128)(2,1)S(1)}, u32[]{:S(2)}, u32[]{:S(2)}) collective-permute-start(bf16[4,1536]{1,0:T(4,128)(2,1)S(1)} %get-tuple-element.8), channel_id=1, source_target_pairs={{4,0},{8,4},{12,8},{16,12},{20,16},{24,20},{28,24},{32,28},{36,32}... | collective-permute-start | bytes 36872 | tf_op jit(solution)/shard_map/ppermute | solution.py:19
  95.8 7.0 %copy-start.4 = (bf16[512,384]{1,0:T(8,128)(2,1)S(1)}, bf16[512,384]{1,0:T(8,128)(2,1)}, u32[]{:S(2)}) copy-start(bf16[512,384]{1,0:T(8,128)(2,1)} %fusion.49) | copy-start | bytes 1179652
  95.8 7.0 %collective-permute-start.2 = (bf16[4,1536]{1,0:T(4,128)(2,1)S(1)}, bf16[4,1536]{1,0:T(4,128)(2,1)S(1)}, u32[]{:S(2)}, u32[]{:S(2)}) collective-permute-start(bf16[4,1536]{1,0:T(4,128)(2,1)S(1)} %get-tuple-element.7), channel_id=1, source_target_pairs={{0,4},{4,8},{8,12},{12,16},{16,20},{20,24},{24,28},{28,32},{32,36}... | collective-permute-start | bytes 36872 | tf_op jit(solution)/shard_map/ppermute | solution.py:18
  105.9 402.6 %all-gather.12.cloned.1.call-start = ((), (), s32[]{:S(2)}) async-start(), calls=%async_computation.3 | async-start | bytes 38338560 | tf_op jit(solution)/shard_map/all_gather | solution.py:64
  140.0 8.4 %collective-permute-start.5 = (bf16[8,1536]{1,0:T(8,128)(2,1)S(1)}, bf16[8,1536]{1,0:T(8,128)(2,1)S(1)}, u32[]{:S(2)}, u32[]{:S(2)}) collective-permute-start(bf16[8,1536]{1,0:T(8,128)(2,1)S(1)} %get-tuple-element.6), channel_id=1, source_target_pairs={{4,0},{8,4},{12,8},{16,12},{20,16},{24,20},{28,24},{32,28},{36,32}... | collective-permute-start | bytes 73736 | tf_op jit(solution)/shard_map/ppermute | solution.py:19
  143.7 7.0 %copy-start.3 = (bf16[512,384]{1,0:T(8,128)(2,1)S(1)}, bf16[512,384]{1,0:T(8,128)(2,1)}, u32[]{:S(2)}) copy-start(bf16[512,384]{1,0:T(8,128)(2,1)} %add_convert_fusion.1) | copy-start | bytes 1179652
  143.7 7.0 %collective-permute-start.4 = (bf16[8,1536]{1,0:T(8,128)(2,1)S(1)}, bf16[8,1536]{1,0:T(8,128)(2,1)S(1)}, u32[]{:S(2)}, u32[]{:S(2)}) collective-permute-start(bf16[8,1536]{1,0:T(8,128)(2,1)S(1)} %get-tuple-element.5), channel_id=1, source_target_pairs={{0,4},{4,8},{8,12},{12,16},{16,20},{20,24},{24,28},{28,32},{32,36}... | collective-permute-start | bytes 73736 | tf_op jit(solution)/shard_map/ppermute | solution.py:18
  150.7 2.4 copy-start.5
  150.7 3.6 copy-start.6
  508.5 14.2 %copy-start.1 = (bf16[512,384]{1,0:T(8,128)(2,1)S(1)}, bf16[512,384]{1,0:T(8,128)(2,1)}, u32[]{:S(2)}) copy-start(bf16[512,384]{1,0:T(8,128)(2,1)} %param.7) | copy-start | bytes 1179652
Sparse Core Ops, SparseCore 0:
  10.5 29.3 all-gather.5
  58.9 28.6 all-gather.7
  106.0 29.3 all-gather.9
  154.4 353.9 all-gather.11
